TPU v7x, 512 devices: a whole 4x8x8 slice. The times are simulated.
512 devices in a mesh: ctx: 64 (over z, x, y_lo), tp: 8 (over y_hi, core).
Axes of the slice: x: 4, y: 8 (y_hi: 4, y_lo: 2; y = y_hi * 2 + y_lo), z: 8, core: 2. Of those that a mesh axis runs over, the one named last changes fastest.
Arguments:
- tokens: bfloat16 [8192, 4096], P('ctx'), may hold values from -6 to 6
- new_token_states: bfloat16 [4, 4096], replicated, may hold values from -6.0625 to 6.0625
- w_query: bfloat16 [4096, 2048], P('ctx', 'tp'), may hold values from -0.12162204 to 0.12162204
- key_matrix: bfloat16 [4096, 1024], P('ctx', 'tp'), may hold values from -0.12162204 to 0.12162204
- value_matrix: bfloat16 [4096, 1024], P('ctx', 'tp'), may hold values from -0.09375 to 0.09375
- w_out: bfloat16 [2048, 4096], P('tp', 'ctx'), may hold values from -0.125 to 0.125
- lengths: int32 [4], replicated, may hold values from 1 to 4096, 8192 in all
- block_map: int32 [128], replicated, may hold values from 0 to 127, each once
Outputs:
- prefill_out: bfloat16 [8192, 4096], P('ctx', 'tp')
- decode_out: bfloat16 [4, 4096], P(None, 'tp')
Inputs may be any that keep to these rules, and one draw needn't show every extreme that they name: The lengths sum to 8192, and some request has exactly 4096 tokens. `block_map`: each of the 128 initial blocks is held exactly once.
All inputs are finite; a program needn't handle non-finite values.
Results may differ from a plain program's by a relative error of at most 0.015.
Values may be sent and summed in bfloat16 or wider, within the bound.
A program may use at most 64 MiB of HBM per device.

v0:
```python
import math
import jax
import jax.numpy as jnp
from jax import lax
from jax.sharding import PartitionSpec as P

HEAD_SIZE = 128
floor_value = -1e30


def initial_positions(block_map, first_row, row_count, block_rows):
    row_ids = first_row + jnp.arange(row_count, dtype=jnp.int32)
    block_ids = row_ids // block_rows
    table_ids = jnp.arange(block_map.shape[0], dtype=jnp.int32)
    mapped = jnp.sum(
        jnp.where(block_ids[:, None] == table_ids[None, :], block_map[None, :], 0), axis=1
    )
    return mapped * block_rows + row_ids % block_rows


def request_index(positions, request_ends):
    return jnp.sum((positions[:, None] >= request_ends[None, :]).astype(jnp.int32), axis=1)


def round_weights(weights):
    rounded = weights.astype(jnp.bfloat16)
    rounded = lax.optimization_barrier(rounded)
    return rounded.astype(jnp.float32)


def softmax_parts(
    dec_heads, projected_key_rows, projected_value_rows, owned, kv_heads, head_dim, score_scale
):
    row_count = projected_key_rows.shape[0]
    scores = (
        jnp.einsum(
            "rgjd,tgd->rgjt",
            dec_heads,
            projected_key_rows.reshape(row_count, kv_heads, head_dim),
            preferred_element_type=jnp.float32,
        )
        * score_scale
    )
    scores = jnp.where(owned, scores, floor_value)
    part_peak = jnp.max(scores, axis=3)
    weights = jnp.where(owned, jnp.exp(scores - part_peak[..., None]), 0.0)
    part_total = jnp.sum(weights, axis=3)
    part_mixed = jnp.einsum(
        "rgjt,tgd->rgjd",
        weights.astype(jnp.bfloat16),
        projected_value_rows.reshape(row_count, kv_heads, head_dim),
        preferred_element_type=jnp.float32,
    )
    return (part_peak, part_total, part_mixed)


def on_device(
    tokens, new_token_states, w_query, key_matrix, value_matrix, w_out, lengths, block_map
):
    local_rows = tokens.shape[0]
    block_rows = local_rows // 2
    request_count = new_token_states.shape[0]
    head_dim = HEAD_SIZE
    query_width = w_query.shape[1]
    kv_width = key_matrix.shape[1]
    kv_heads = kv_width // head_dim
    query_group_count = query_width // kv_width
    score_scale = 1.0 / math.sqrt(head_dim)
    device = lax.axis_index("ctx")
    request_ends = jnp.cumsum(lengths)
    inputs = jnp.concatenate([tokens, new_token_states], axis=0)
    joined = lax.all_gather(
        jnp.concatenate([w_query, key_matrix, value_matrix, w_out.T], axis=1),
        "ctx",
        axis=0,
        tiled=True,
    )
    qkv_width = query_width + 2 * kv_width
    projected_all = jnp.dot(
        inputs, joined[:, :qkv_width], preferred_element_type=jnp.float32
    ).astype(jnp.bfloat16)
    out_weight = joined[:, qkv_width:].T
    query_all = projected_all[:, :query_width]
    key_all = projected_all[:, query_width : query_width + kv_width]
    value_all = projected_all[:, query_width + kv_width :]
    local_query = query_all[:local_rows]
    local_keys = key_all[:local_rows]
    local_values = value_all[:local_rows]
    dec_query = query_all[local_rows:]
    decode_key_rows = key_all[local_rows:]
    decode_value_rows = value_all[local_rows:]
    token_pos = initial_positions(block_map, device * local_rows, local_rows, block_rows)
    token_request = request_index(token_pos, request_ends)
    query_heads = local_query.reshape(local_rows, kv_heads, query_group_count, head_dim)

    def attend(running, shard_pieces, first_row):
        peak_run, total_run, mixed_run = running
        key_piece, value_piece = shard_pieces
        row_count = key_piece.shape[0]
        key_pos = initial_positions(block_map, first_row, row_count, block_rows)
        key_request = request_index(key_pos, request_ends)
        allowed = (key_request[None, :] == token_request[:, None]) & (
            key_pos[None, :] <= token_pos[:, None]
        )
        scores = (
            jnp.einsum(
                "tgjd,kgd->gjtk",
                query_heads,
                key_piece.reshape(row_count, kv_heads, head_dim),
                preferred_element_type=jnp.float32,
            )
            * score_scale
        )
        scores = jnp.where(allowed, scores, floor_value)
        peak_new = jnp.maximum(peak_run, jnp.max(scores, axis=3))
        weights = jnp.where(allowed, jnp.exp(scores - peak_new[..., None]), 0.0)
        rescale = jnp.exp(peak_run - peak_new)
        total_new = total_run * rescale + jnp.sum(weights, axis=3)
        mixed_new = mixed_run * rescale[..., None] + jnp.einsum(
            "gjtk,kgd->gjtd",
            weights.astype(jnp.bfloat16),
            value_piece.reshape(row_count, kv_heads, head_dim),
            preferred_element_type=jnp.float32,
        )
        return (peak_new, total_new, mixed_new)

    start_state = (
        jnp.full((kv_heads, query_group_count, local_rows), floor_value, jnp.float32),
        jnp.zeros((kv_heads, query_group_count, local_rows), jnp.float32),
        jnp.zeros((kv_heads, query_group_count, local_rows, head_dim), jnp.float32),
    )
    dec_heads = dec_query.reshape(request_count, kv_heads, query_group_count, head_dim)
    request_ids = jnp.arange(request_count, dtype=jnp.int32)
    cache_both = lax.all_gather(
        jnp.concatenate([local_keys, local_values], axis=1), "ctx", axis=0, tiled=True
    )
    cache_keys = cache_both[:, :kv_width]
    cache_values = cache_both[:, kv_width:]
    total_rows = cache_keys.shape[0]
    shard_count = total_rows // local_rows
    limit = max(1, 1024 // local_rows)
    step_rows = local_rows * math.gcd(shard_count, 1 << limit.bit_length() - 1)

    def key_step(running, step_index):
        first_row = step_index * step_rows
        pieces = (
            lax.dynamic_slice_in_dim(cache_keys, first_row, step_rows, 0),
            lax.dynamic_slice_in_dim(cache_values, first_row, step_rows, 0),
        )
        return (attend(running, pieces, first_row), None)

    final_state, unused = lax.scan(
        key_step, start_state, jnp.arange(total_rows // step_rows, dtype=jnp.int32)
    )
    peak_run, total_run, mixed_run = final_state
    cache_pos = (
        block_map[:, None] * block_rows + jnp.arange(block_rows, dtype=jnp.int32)[None, :]
    ).reshape(total_rows)
    cache_request = request_index(cache_pos, request_ends)
    owned = (cache_request[None, :] == request_ids[:, None])[:, None, None, :]
    cache_peak, cache_total, cache_mixed = softmax_parts(
        dec_heads, cache_keys, cache_values, owned, kv_heads, head_dim, score_scale
    )
    attended = (
        (mixed_run / total_run[..., None]).transpose(2, 0, 1, 3).reshape(local_rows, query_width)
    )
    attended = attended.astype(jnp.bfloat16)
    own_keys = decode_key_rows.reshape(request_count, kv_heads, 1, head_dim).astype(jnp.float32)
    own_values = decode_value_rows.reshape(request_count, kv_heads, 1, head_dim).astype(jnp.float32)
    self_scores = jnp.sum(dec_heads.astype(jnp.float32) * own_keys, axis=3) * score_scale
    peak_all = jnp.maximum(cache_peak, self_scores)
    rescale = jnp.exp(cache_peak - peak_all)
    self_weights = jnp.exp(self_scores - peak_all)
    dec_total = cache_total * rescale + self_weights
    dec_mixed = (
        cache_mixed * rescale[..., None] + round_weights(self_weights)[..., None] * own_values
    )
    dec_attn = (
        (dec_mixed / dec_total[..., None]).reshape(request_count, query_width).astype(jnp.bfloat16)
    )
    attended_all = jnp.concatenate([attended, dec_attn], axis=0)
    projected = jnp.dot(attended_all, out_weight, preferred_element_type=jnp.float32)
    summed_rows = lax.psum_scatter(
        projected.astype(jnp.bfloat16), "tp", scatter_dimension=1, tiled=True
    ).astype(jnp.float32)
    summed_rows = summed_rows.astype(jnp.bfloat16)
    return (summed_rows[:local_rows], summed_rows[local_rows:])


def solution(mesh):
    return jax.shard_map(
        on_device,
        mesh=mesh,
        in_specs=(
            P("ctx", None),
            P(),
            P("ctx", "tp"),
            P("ctx", "tp"),
            P("ctx", "tp"),
            P("tp", "ctx"),
            P(),
            P(),
        ),
        out_specs=(P("ctx", "tp"), P(None, "tp")),
        check_vma=False,
    )
```

profile of v0, /device:TPU:17, one launch (start us, length us, event | category | flops | bytes accessed | tf_op | source)
XLA Modules:
  0.0 756.4 jit_solution(10160451759107932689)
XLA Ops:
  7.2 1.5 pad_maximum_fusion
  8.8 288.3 %all-gather.3.cloned.1.call-done = bf16[4096,768]{1,0:T(8,128)(2,1)} async-done(((bf16[64,768]{1,0:T(8,128)(2,1)}), bf16[4096,768]{1,0:T(8,128)(2,1)}) %all-gather.3.cloned.1.call-update) | async-done | bytes 6291472 | tf_op jit(solution)/shard_map/all_gather | solution.py:72
  297.0 3.3 fusion.33
  300.3 0.6 fusion.85
  301.2 0.7 broadcast_multiply_fusion
  302.1 0.8 select_reduce_fusion.1
  302.9 0.6 fusion.77
  303.5 1.3 convert_reduce_fusion.2
  305.2 308.1 %all-gather.5.cloned.1.call-done = bf16[8192,256]{1,0:T(8,128)(2,1)} async-done(((bf16[128,256]{1,0:T(8,128)(2,1)}), bf16[8192,256]{1,0:T(8,128)(2,1)}) %all-gather.5.cloned.1.call-update) | async-done | bytes 4194320 | tf_op jit(solution)/shard_map/all_gather | solution.py:134
  613.3 2.3 fusion.86
  615.6 0.3 fusion.60
  615.9 2.0 fusion.57
  618.2 3.8 fusion.84
  622.0 43.6 %while.17 = (s32[]{:T(128)}, f32[1,2,128]{2,1,0:T(2,128)S(1)}, f32[1,2,128]{2,1,0:T(2,128)S(1)}, f32[1,2,128,128]{3,2,1,0:T(8,128)S(1)}, s32[8]{0:T(128)S(1)}, /...) while((s32[]{:T(128)}, f32[1,2,128]{2,1,0:T(2,128)S(1)}, ...), condition=%wide.region_8.9_spmd.clone, body=%wide.region_3.8_spmd.clone.sunk | while | flops 137504256 | bytes 4577331 | solution.py:152
  622.0 0.6 dynamic_slice.37
  623.2 1.0 select_reduce_fusion.3
  624.3 1.0 compare_and_fusion.2
  625.4 0.3 fusion.97
  625.7 1.4 fusion.100
  627.4 0.6 dynamic_slice.37
  628.7 1.0 select_reduce_fusion.3
  629.8 1.0 compare_and_fusion.2
  630.8 0.3 fusion.97
  631.2 1.4 fusion.100
  632.6 0.2 fusion.99
  632.9 0.6 dynamic_slice.37
  634.1 1.0 select_reduce_fusion.3
  635.2 1.0 compare_and_fusion.2
  636.3 0.3 fusion.97
  636.7 1.4 fusion.100
  638.0 0.2 fusion.99
  638.3 0.6 dynamic_slice.37
  639.6 1.0 select_reduce_fusion.3
  640.7 1.0 compare_and_fusion.2
  641.7 0.3 fusion.97
  642.1 1.4 fusion.100
  643.5 0.2 fusion.99
  643.8 0.6 dynamic_slice.37
  645.0 1.0 select_reduce_fusion.3
  646.2 1.0 compare_and_fusion.2
  647.2 0.3 fusion.97
  647.6 1.4 fusion.100
  648.9 0.2 fusion.99
  649.2 0.6 dynamic_slice.37
  650.5 1.0 select_reduce_fusion.3
  651.6 1.0 compare_and_fusion.2
  652.6 0.3 fusion.97
  653.0 1.4 fusion.100
  654.4 0.2 fusion.99
  654.7 0.6 dynamic_slice.37
  656.0 1.0 select_reduce_fusion.3
  657.1 1.0 compare_and_fusion.2
  658.1 0.3 fusion.97
  658.5 1.4 fusion.100
  659.9 0.2 fusion.99
  660.2 0.6 dynamic_slice.37
  661.4 1.0 select_reduce_fusion.3
  662.5 1.0 compare_and_fusion.2
  663.6 0.3 fusion.97
  663.9 1.4 fusion.100
  665.7 3.5 convolution_convert_fusion
  669.2 77.8 %reduce-scatter.2.cloned.1.call-done = bf16[132,512]{1,0:T(8,128)(2,1)} async-done(((bf16[132,4096]{1,0:T(8,128)(2,1)}), bf16[132,512]{1,0:T(8,128)(2,1)}) %reduce-scatter.2.cloned.1.call-update) | async-done | bytes 135184 | tf_op jit(solution)/shard_map/reduce_scatter | solution.py:183
  747.0 1.6 slice.60
  748.6 1.3 slice.61
  (113 shorter events, 2.8 us)
Async XLA Ops:
  7.2 289.9 %all-gather.3.cloned.1.call-start = ((), (), s32[]{:S(2)}) async-start(), calls=%async_computation.1 | async-start | bytes 6389760 | tf_op jit(solution)/shard_map/all_gather | solution.py:72
  8.7 292.4 %copy-start = (s32[4]{0:T(128)S(1)}, s32[4]{0:T(128)}, u32[]{:S(2)}) copy-start(s32[4]{0:T(128)} %param.16) | copy-start | bytes 52
  8.7 604.6 %all-gather.5.cloned.1.call-start = ((), (), s32[]{:S(2)}) async-start(), calls=%async_computation.2 | async-start | bytes 4259840 | tf_op jit(solution)/shard_map/all_gather | solution.py:134
  301.0 446.0 %reduce-scatter.2.cloned.1.call-start = ((), (), s32[]{:S(2)}) async-start(), calls=%async_computation.3 | async-start | bytes 1253376 | tf_op jit(solution)/shard_map/reduce_scatter | solution.py:183
  622.0 3.4 copy-start.1
  625.7 1.6 copy-start.2
  627.4 3.4 copy-start.1
  631.2 1.6 copy-start.2
  632.9 3.4 copy-start.1
  636.6 1.6 copy-start.2
  638.3 3.4 copy-start.1
  642.1 1.6 copy-start.2
  643.8 3.4 copy-start.1
  647.6 1.6 copy-start.2
  649.2 3.4 copy-start.1
  653.0 1.6 copy-start.2
  654.7 3.4 copy-start.1
  658.5 1.6 copy-start.2
  660.1 3.4 copy-start.1
  663.9 1.6 copy-start.2
Sparse Core Ops, SparseCore 0:
  10.7 286.3 all-gather.2
  301.1 312.1 all-gather.4
  669.3 77.5 reduce-scatter.1
where the time goes:
time: 757 us; the launch traced here: 756 us
  waiting for transfers between devices  674 us (89%)
  matrix products  24.9 us (3%)
  other arithmetic  24.7 us (3%)
  between operations  13.9 us (2%)
  local copies, waits for them, and re-layouts  12.5 us (2%)
    all_gather x1, waiting for transfers between devices, on_device(): lax.all_gather(jnp.concatenate([local_keys, local_values], axis=1), 'ctx'...  308 us
    all_gather x1, waiting for transfers between devices, on_device(): lax.all_gather(jnp.concatenate([w_query, key_matrix, value_matrix, w_out....  288 us
    reduce_scatter x1, waiting for transfers between devices, on_device(): lax.psum_scatter(projected.astype(jnp.bfloat16), 'tp', scatter_dimension=...  77.8 us
  transfers between devices with their start and end apart: 3, of which 3 were waited for; matrix products, arithmetic and copies ran while one was open for 1% of the time, Pallas kernels for 0%

commit v1 on v0

--- a/solution.py
+++ b/solution.py
@@ -69,12 +69,9 @@
     device = lax.axis_index("ctx")
     request_ends = jnp.cumsum(lengths)
     inputs = jnp.concatenate([tokens, new_token_states], axis=0)
-    joined = lax.all_gather(
-        jnp.concatenate([w_query, key_matrix, value_matrix, w_out.T], axis=1),
-        "ctx",
-        axis=0,
-        tiled=True,
-    )
+    x = jnp.concatenate([w_query, key_matrix, value_matrix, w_out.T], axis=1)
+    sent = jnp.stack([x] * lax.axis_size("ctx"))
+    joined = jnp.concatenate(lax.all_to_all(sent, "ctx", 0, 0), axis=0)
     qkv_width = query_width + 2 * kv_width
     projected_all = jnp.dot(
         inputs, joined[:, :qkv_width], preferred_element_type=jnp.float32

time: 757 us -> 584 us (0.77)
  waiting for transfers between devices: 674 us -> 348 us
  blocking collectives: 0 us -> 153 us
    all_gather x1 -> x0, waiting for transfers between devices: 288 us -> none  [on_device(): lax.all_gather(jnp.concatenate([w_query, key_matrix, value_matrix, w_out....]
    all_to_all x0 -> x1, blocking collectives: none -> 153 us  [on_device(): joined = jnp.concatenate(lax.all_to_all(sent, 'ctx', 0, 0), axis=0)]
    all_gather x1, waiting for transfers between devices: 308 us -> 270 us  [on_device(): lax.all_gather(jnp.concatenate([local_keys, local_values], axis=1), 'ctx'...]
  transfers between devices with their start and end apart: 3 -> 2, of which waited for: 3 -> 2; matrix products, arithmetic and copies ran while one was open for 1% -> 1% of each run, Pallas kernels for 0% -> 0%
where the time goes in v1:
time: 584 us; the launch traced here: 583 us
  waiting for transfers between devices  348 us (60%)
  blocking collectives  153 us (26%)
  other arithmetic  24.1 us (4%)
  matrix products  22.4 us (4%)
  local copies, waits for them, and re-layouts  15.2 us (3%)
  between operations  14.2 us (2%)
  loops' own time  6.07 us (1%)
    all_gather x1, waiting for transfers between devices, on_device(): lax.all_gather(jnp.concatenate([local_keys, local_values], axis=1), 'ctx'...  270 us
    all_to_all x1, blocking collectives, on_device(): joined = jnp.concatenate(lax.all_to_all(sent, 'ctx', 0, 0), axis=0)  153 us
    reduce_scatter x1, waiting for transfers between devices, on_device(): lax.psum_scatter(projected.astype(jnp.bfloat16), 'tp', scatter_dimension=...  77.9 us
  transfers between devices with their start and end apart: 2, of which 2 were waited for; matrix products, arithmetic and copies ran while one was open for 1% of the time, Pallas kernels for 0%

profile of v1, /device:TPU:17, one launch (start us, length us, event | category | flops | bytes accessed | tf_op | source)
XLA Modules:
  0.0 583.4 jit_solution(3903232740004640046)
XLA Ops:
  7.2 0.8 pad_maximum_fusion
  8.0 0.8 stack.2
  8.8 153.5 %all_to_all.5 = bf16[64,64,768]{2,1,0:T(8,128)(2,1)S(1)} all-to-all(bf16[64,64,768]{2,1,0:T(8,128)(2,1)S(1)} %stack.2), channel_id=1, replica_groups=mesh['ctx'=64,'tp'=8] {'ctx'}, dimensions={0} | all-to-all | bytes 12582912 | tf_op jit(solution)/shard_map/all_to_all | solution.py:74
  162.3 0.8 fusion.33
  163.1 1.9 copy-done
  164.9 0.6 fusion.85
  165.9 0.7 broadcast_multiply_fusion
  166.7 0.8 select_reduce_fusion.1
  167.5 0.6 fusion.77
  168.1 1.3 convert_reduce_fusion.2
  169.9 270.0 %all-gather.2.cloned.1.call-done = bf16[8192,256]{1,0:T(8,128)(2,1)} async-done(((bf16[128,256]{1,0:T(8,128)(2,1)}), bf16[8192,256]{1,0:T(8,128)(2,1)}) %all-gather.2.cloned.1.call-update) | async-done | bytes 4194320 | tf_op jit(solution)/shard_map/all_gather | solution.py:131
  439.8 2.3 fusion.86
  442.2 0.3 fusion.60
  442.5 2.0 fusion.57
  444.7 3.8 fusion.84
  448.5 43.6 %while.17 = (s32[]{:T(128)}, f32[1,2,128]{2,1,0:T(2,128)S(1)}, f32[1,2,128]{2,1,0:T(2,128)S(1)}, f32[1,2,128,128]{3,2,1,0:T(8,128)S(1)}, s32[8]{0:T(128)S(1)}, /...) while((s32[]{:T(128)}, f32[1,2,128]{2,1,0:T(2,128)S(1)}, ...), condition=%wide.region_8.9_spmd.clone, body=%wide.region_3.8_spmd.clone.sunk | while | flops 137504256 | bytes 4577331 | solution.py:149
  448.5 0.6 dynamic_slice.37
  449.8 1.0 select_reduce_fusion.3
  450.9 1.0 compare_and_fusion.2
  451.9 0.4 fusion.97
  452.3 1.4 fusion.100
  453.7 0.2 fusion.99
  454.0 0.6 dynamic_slice.37
  455.2 1.0 select_reduce_fusion.3
  456.3 1.0 compare_and_fusion.2
  457.4 0.3 fusion.97
  457.8 1.4 fusion.100
  459.1 0.2 fusion.99
  459.4 0.6 dynamic_slice.37
  460.7 1.0 select_reduce_fusion.3
  461.8 1.0 compare_and_fusion.2
  462.8 0.3 fusion.97
  463.2 1.4 fusion.100
  464.6 0.2 fusion.99
  464.9 0.6 dynamic_slice.37
  466.1 1.0 select_reduce_fusion.3
  467.3 1.0 compare_and_fusion.2
  468.3 0.3 fusion.97
  468.7 1.4 fusion.100
  470.1 0.2 fusion.99
  470.3 0.6 dynamic_slice.37
  471.6 1.0 select_reduce_fusion.3
  472.7 1.0 compare_and_fusion.2
  473.8 0.3 fusion.97
  474.1 1.4 fusion.100
  475.8 0.6 dynamic_slice.37
  477.1 1.0 select_reduce_fusion.3
  478.2 1.0 compare_and_fusion.2
  479.2 0.3 fusion.97
  479.6 1.4 fusion.100
  481.3 0.6 dynamic_slice.37
  482.5 1.0 select_reduce_fusion.3
  483.6 1.0 compare_and_fusion.2
  484.7 0.3 fusion.97
  485.0 1.4 fusion.100
  486.7 0.6 dynamic_slice.37
  488.0 1.0 select_reduce_fusion.3
  489.1 1.0 compare_and_fusion.2
  490.1 0.3 fusion.97
  490.5 1.4 fusion.100
  492.3 3.5 convolution_convert_fusion
  495.8 77.9 %reduce-scatter.2.cloned.1.call-done = bf16[132,512]{1,0:T(8,128)(2,1)} async-done(((bf16[132,4096]{1,0:T(8,128)(2,1)}), bf16[132,512]{1,0:T(8,128)(2,1)}) %reduce-scatter.2.cloned.1.call-update) | async-done | bytes 135184 | tf_op jit(solution)/shard_map/reduce_scatter | solution.py:180
  573.7 1.6 slice.60
  575.3 1.3 slice.61
  (118 shorter events, 3.2 us)
Async XLA Ops:
  7.2 432.7 %all-gather.2.cloned.1.call-start = ((), (), s32[]{:S(2)}) async-start(), calls=%async_computation.2 | async-start | bytes 4259840 | tf_op jit(solution)/shard_map/all_gather | solution.py:131
  8.8 153.5 %copy-start.1 = (bf16[128,4096]{1,0:T(8,128)(2,1)S(1)}, bf16[128,4096]{1,0:T(8,128)(2,1)}, u32[]{:S(2)}) copy-start(bf16[128,4096]{1,0:T(8,128)(2,1)} %param.10) | copy-start | bytes 3145732
  8.8 153.5 %copy-start.2 = (bf16[4,4096]{1,0:T(4,128)(2,1)S(1)}, bf16[4,4096]{1,0:T(4,128)(2,1)}, u32[]{:S(2)}) copy-start(bf16[4,4096]{1,0:T(4,128)(2,1)} %param.11) | copy-start | bytes 98308
  162.3 2.7 copy-start
  162.3 3.4 copy-start.3
  165.6 408.1 %reduce-scatter.2.cloned.1.call-start = ((), (), s32[]{:S(2)}) async-start(), calls=%async_computation.3 | async-start | bytes 1253376 | tf_op jit(solution)/shard_map/reduce_scatter | solution.py:180
  448.5 3.4 copy-start.4
  452.3 1.6 copy-start.5
  454.0 3.4 copy-start.4
  457.7 1.6 copy-start.5
  459.4 3.4 copy-start.4
  463.2 1.6 copy-start.5
  464.9 3.4 copy-start.4
  468.7 1.6 copy-start.5
  470.3 3.4 copy-start.4
  474.1 1.6 copy-start.5
  475.8 3.4 copy-start.4
  479.6 1.6 copy-start.5
  481.2 3.4 copy-start.4
  485.0 1.6 copy-start.5
  486.7 3.4 copy-start.4
  490.5 1.6 copy-start.5
Sparse Core Ops, SparseCore 0:
  165.7 274.0 all-gather.1
  495.9 77.7 reduce-scatter.1
